TPU v7x, 1024 devices: a whole 4x4x32 slice. The times are simulated.
1024 devices in a mesh: shell: 8 (over x, core), tile: 128 (over z, y).
Axes of the slice: x: 4, y: 4, z: 32, core: 2. Of those that a mesh axis runs over, the one named last changes fastest.
Arguments:
- residual: bfloat16 [32, 2097152], P('shell', 'tile'), may hold values from -6 to 6
- tile_ray: int32 [16384], P('tile'), may hold values from 0 to 127, as said below
- filter_rows: bfloat16 [128, 128], replicated, may hold values from -0.5 to 0.5
- filter_cols: bfloat16 [128, 128], replicated, may hold values from -0.5 to 0.5
- band_lo: int32 [32], replicated, may hold values from 0 to 16
- shell_weight: float32 [32], replicated, may hold values from 0.3 to 3
Outputs:
- shell_grad: bfloat16 [32, 2097152], P('shell', 'tile')
Inputs may be any that keep to these rules, and one draw needn't show every extreme that they name: `tile_ray`: for each tile t, entries t * 128 to (t + 1) * 128 - 1 are a permutation of 0 to 127.
All inputs are finite; a program needn't handle non-finite values.
Results may differ from a plain program's by a relative error of at most 0.006.
Values may be sent and summed in bfloat16 or wider, within the bound.
No kernel may reach another device: no remote copies, remote signals or barrier semaphores. Data moves between devices by JAX's collectives and lax.ppermute only.
A program may use at most 32 MiB of HBM per device.

v0:
```python
import jax
import jax.numpy as jnp
from jax import lax
from jax.sharding import PartitionSpec as P


def kernel_table(band_lo, shell_weight):
    count = shell_weight.shape[0]
    band = count // 2
    index = jnp.arange(count)
    chi_shell = (index.astype(jnp.float32) + 0.5) / count
    chi_source = (band_lo.astype(jnp.float32) + band) / count
    inside = (index[None, :] >= band_lo[:, None]) & (index[None, :] < band_lo[:, None] + band)
    values = (
        8.0
        * shell_weight[None, :]
        * chi_shell[None, :]
        * (chi_source[:, None] - chi_shell[None, :])
        / chi_source[:, None]
    )
    return jnp.where(inside, values, jnp.zeros_like(values)).astype(jnp.bfloat16)


def shards(residual, tile_ray, filter_rows, filter_cols, band_lo, shell_weight):
    planes, rays = residual.shape
    ntile = lax.axis_size("tile")
    run = rays // ntile
    grouped = residual.reshape(planes, ntile, run)
    arrived = lax.all_to_all(grouped, "tile", split_axis=1, concat_axis=1, tiled=True)
    image = jnp.take(arrived, tile_ray, axis=1)
    half = jnp.einsum("sik,kb->sib", image, filter_cols, preferred_element_type=jnp.float32)
    whole = lax.dot_general(
        half,
        filter_rows.astype(jnp.float32),
        (((1,), (0,)), ((), ())),
        precision=lax.Precision.HIGHEST,
    )
    smoothed = jnp.swapaxes(whole, 1, 2).astype(jnp.bfloat16).reshape(planes, rays)
    kernel = kernel_table(band_lo, shell_weight)
    mine = lax.axis_index("shell")
    own_rows = lax.dynamic_slice_in_dim(kernel, mine * planes, planes, 0)
    shell_grad = lax.psum_scatter(
        jnp.dot(own_rows.T, smoothed, preferred_element_type=jnp.float32),
        "shell",
        scatter_dimension=0,
        tiled=True,
    )
    return shell_grad.astype(jnp.bfloat16)


def solution(mesh):
    in_specs = (P("shell", "tile"), P("tile"), P(), P(), P(), P())
    out_specs = P("shell", "tile")
    return jax.shard_map(shards, mesh=mesh, in_specs=in_specs, out_specs=out_specs, check_vma=False)
```

profile of v0, /device:TPU:1, one launch (start us, length us, event | category | flops | bytes accessed | tf_op | source)
XLA Modules:
  0.0 119.1 jit_solution(12792568411217018098)
XLA Ops:
  0.0 0.0 copy-start
  0.0 33.9 %all-to-all-start = ((bf16[4,128,128]{2,0,1:T(4,128)(2,1)}), bf16[4,128,128]{2,0,1:T(4,128)(2,1)S(1)}, u32[]{:S(2)}, u32[]{:S(2)}) async-start(bf16[4,128,128]{2,0,1:T(4,128)(2,1)} %bitcast.18), calls=%async_computation | async-start | bytes 262144 | tf_op jit(solution)/shard_map/all_to_all | solution.py:29
  33.9 0.7 add_multiply_fusion
  34.5 0.7 dynamic-slice.3
  35.3 0.1 dynamic-slice.2
  35.3 0.7 broadcast_add_fusion
  36.0 0.1 dynamic-slice.4
  36.1 1.3 %dynamic-slice = u32[1]{0:T(128)} dynamic-slice(u32[1024]{0:T(1024)} %constant.43, u32[]{:T(128)S(6)} %add.48), dynamic_slice_sizes={1} | dynamic-slice | bytes 12
  38.0 0.7 compare_select_fusion
  38.7 0.7 compare_and_fusion
  39.3 0.7 add_multiply_fusion.1
  40.0 19.3 %all-to-all-done = bf16[4,128,128]{2,0,1:T(4,128)(2,1)S(1)} async-done(((bf16[4,128,128]{2,0,1:T(4,128)(2,1)}), bf16[4,128,128]{2,0,1:T(4,128)(2,1)S(1)}, u32[]{:S(2)}, u32[]{:S(2)}) %all-to-all-start) | async-done | bytes 131104 | tf_op jit(solution)/shard_map/all_to_all | solution.py:29
  59.3 0.7 gather_fusion
  60.0 0.2 select_bitcast_fusion
  60.3 0.0 copy-done
  60.3 0.2 fusion.4
  60.5 1.0 fusion
  61.5 0.1 copy.10
  61.7 0.6 fusion.1
  62.2 56.1 %all-reduce.2 = bf16[32,16384]{1,0:T(8,128)(2,1)S(1)} all-reduce(f32[32,16384]{1,0:T(8,128)S(1)} %fusion.1), channel_id=2, replica_groups=mesh['shell'=8,'tile'=128] {'shell'}, use_global_device_ids=true, to_apply=%region_0.1.clone | all-reduce | flops 524288 | bytes 3145728
  118.4 0.7 dynamic-slice_convert_fusion
  (1 shorter events, 0.0 us)
Async XLA Ops:
  0.0 60.3 %copy-start = (bf16[128,128]{1,0:T(8,128)(2,1)S(1)}, bf16[128,128]{1,0:T(8,128)(2,1)}, u32[]{:S(2)}) copy-start(bf16[128,128]{1,0:T(8,128)(2,1)} %param.9) | copy-start | bytes 98308
  0.0 59.3 %all-to-all-start = ((bf16[4,128,128]{2,0,1:T(4,128)(2,1)}), bf16[4,128,128]{2,0,1:T(4,128)(2,1)S(1)}, u32[]{:S(2)}, u32[]{:S(2)}) async-start(bf16[4,128,128]{2,0,1:T(4,128)(2,1)} %bitcast.18), calls=%async_computation | async-start | bytes 262144 | tf_op jit(solution)/shard_map/all_to_all | solution.py:29
where the time goes:
time: 121 us; the launch traced here: 119 us
  blocking collectives  56.1 us (46%)
  starting transfers between devices  33.9 us (28%)
  waiting for transfers between devices  19.3 us (16%)
  local copies, waits for them, and re-layouts  3.76 us (3%)
  other arithmetic  3.51 us (3%)
  matrix products  1.81 us (1%)
    unnamed x1, blocking collectives  56.1 us
    all_to_all x1, starting transfers between devices, shards(): lax.all_to_all(grouped, 'tile', split_axis=1, concat_axis=1, tiled=True)  33.9 us
    all_to_all x1, waiting for transfers between devices, shards(): lax.all_to_all(grouped, 'tile', split_axis=1, concat_axis=1, tiled=True)  19.3 us
  transfers between devices with their start and end apart: 1, of which 1 were waited for; matrix products, arithmetic and copies ran while one was open for 5% of the time, Pallas kernels for 0%

commit v1 on v0

v1 whole, which is shorter than its diff:
```python
import jax
import jax.numpy as jnp
from jax import lax
from jax.experimental import pallas as pl
from jax.experimental.pallas import tpu as pltpu
from jax.sharding import PartitionSpec as P

VMEM = pl.BlockSpec(memory_space=pltpu.VMEM)
TRIM = pltpu.CompilerParams(vmem_limit_bytes=16 * 2**20)
ROW_BY_ROW = (((1,), (1,)), ((), ()))


def iota(shape, axis):
    return lax.broadcasted_iota(jnp.int32, shape, axis)


def tables_kernel(groups, band_ref, weight_ref, ray_ref, rows_ref, mix_ref, smooth_ref):
    count = band_ref.shape[1]
    per = count // groups
    band = count // 2
    size = mix_ref.shape[0]
    run = size // groups
    shell = iota((count, count), 0)
    plane = iota((count, count), 1)
    low = jnp.broadcast_to(band_ref[...], (count, count))
    lanes = jnp.broadcast_to(weight_ref[...], (count, count))
    weight = jnp.sum(jnp.where(shell == plane, lanes, 0.0), axis=1, keepdims=True)
    chi_shell = (shell.astype(jnp.float32) + 0.5) / count
    chi_source = (low.astype(jnp.float32) + band) / count
    values = 8.0 * weight * chi_shell * (chi_source - chi_shell) / chi_source
    inside = (shell >= low) & (shell < low + band)
    table = jnp.where(inside, values, 0.0).astype(jnp.bfloat16)
    spot = iota((size, count), 0)
    pick = (iota((size, count), 1) == spot // run * per + spot % per).astype(jnp.bfloat16)
    by_shell = jnp.dot(pick, table, preferred_element_type=jnp.float32).astype(jnp.bfloat16)
    full = lax.dot_general(by_shell, pick, ROW_BY_ROW, preferred_element_type=jnp.float32)
    here, there = iota((size, size), 0), iota((size, size), 1)
    mix_ref[...] = jnp.where(here % run // per == there % run // per, full, 0.0).astype(jnp.bfloat16)

    side = rows_ref.shape[0]
    each = smooth_ref.shape[0] // side
    wide = iota((side * each, side), 0) // each
    pixel = (iota((side * each, side), 1) == wide).astype(jnp.bfloat16)
    spread = lax.dot_general(pixel, rows_ref[...], ROW_BY_ROW, preferred_element_type=jnp.float32).astype(jnp.bfloat16)
    source = (ray_ref[...] == wide).astype(jnp.bfloat16)
    product = lax.dot_general(spread, source, ROW_BY_ROW, preferred_element_type=jnp.float32)
    smooth_ref[...] = jnp.where(here % each == there % each, product, 0.0).astype(jnp.bfloat16)


def mix_kernel(mix_ref, planes_ref, out_ref):
    out_ref[...] = jnp.dot(mix_ref[...], planes_ref[...], preferred_element_type=jnp.float32).astype(jnp.bfloat16)


def smooth_kernel(smooth_ref, cols_ref, pixels_ref, out_ref):
    half = jnp.dot(pixels_ref[...], cols_ref[...], preferred_element_type=jnp.float32)
    upper = half.astype(jnp.bfloat16)
    lower = (half - upper.astype(jnp.float32)).astype(jnp.bfloat16)
    whole = jnp.dot(smooth_ref[...], upper, preferred_element_type=jnp.float32)
    whole += jnp.dot(smooth_ref[...], lower, preferred_element_type=jnp.float32)
    out_ref[...] = whole.astype(jnp.bfloat16)


def shards(residual, tile_ray, filter_rows, filter_cols, band_lo, shell_weight):
    planes, rays = residual.shape
    groups = lax.axis_size("shell")
    ntile = lax.axis_size("tile")
    run = rays // ntile
    lines = planes * ntile
    square = jax.ShapeDtypeStruct((lines, lines), jnp.bfloat16)
    slab = jax.ShapeDtypeStruct((lines, run), jnp.bfloat16)

    mix, smooth = pl.pallas_call(
        lambda *refs: tables_kernel(groups, *refs), out_shape=(square, square), in_specs=[VMEM] * 4, out_specs=(VMEM, VMEM), compiler_params=TRIM, name="tables"
    )(band_lo.reshape(1, -1), shell_weight.reshape(1, -1), tile_ray.reshape(1, -1), filter_rows)

    by_tile = residual.reshape(planes, groups, ntile // groups, run)
    spread = lax.all_to_all(by_tile, "shell", 1, 1, tiled=True).transpose(1, 2, 0, 3).reshape(lines, run)
    mixed = pl.pallas_call(mix_kernel, out_shape=slab, in_specs=[VMEM] * 2, out_specs=VMEM, compiler_params=TRIM, name="mix")(mix, spread)
    own = lax.all_to_all(mixed.reshape(groups, lines // groups, run), "shell", 0, 0, tiled=True)
    pixels = lax.all_to_all(own.reshape(ntile, planes, run), "tile", 0, 0, tiled=True)
    whole = pl.pallas_call(smooth_kernel, out_shape=slab, in_specs=[VMEM] * 3, out_specs=VMEM, compiler_params=TRIM, name="smooth")(smooth, filter_cols, pixels.reshape(lines, run))
    return whole.reshape(ntile, planes, run).transpose(1, 0, 2).reshape(planes, rays)


def solution(mesh):
    in_specs = (P("shell", "tile"), P("tile"), P(), P(), P(), P())
    out_specs = P("shell", "tile")
    return jax.shard_map(shards, mesh=mesh, in_specs=in_specs, out_specs=out_specs, check_vma=False)
```

time: 121 us -> 84.7 us (0.70)
  the two profiles are of different devices: /device:TPU:1 before, /device:TPU:32 now
where the time goes in v1:
time: 84.7 us; the launch traced here: 84.3 us
  blocking collectives  72.2 us (85%)
  waiting for transfers between devices  4.64 us (5%)
  starting transfers between devices  4.43 us (5%)
  Pallas kernels  2.35 us (3%)
    all_to_all x1, blocking collectives, shards(): lax.all_to_all(own.reshape(ntile, planes, run), 'tile', 0, 0, tiled=True)  63.7 us
    all_to_all x1, blocking collectives, shards(): lax.all_to_all(mixed.reshape(groups, lines // groups, run), 'shell', 0, 0...  8.49 us
    all_to_all x1, waiting for transfers between devices, shards(): lax.all_to_all(by_tile, 'shell', 1, 1, tiled=True).transpose(1, 2, 0, 3)  4.64 us
    all_to_all x1, starting transfers between devices, shards(): lax.all_to_all(by_tile, 'shell', 1, 1, tiled=True).transpose(1, 2, 0, 3)  4.43 us
  transfers between devices with their start and end apart: 1, of which 1 were waited for; matrix products, arithmetic and copies ran while one was open for 0% of the time, Pallas kernels for 1%

profile of v1, /device:TPU:32, one launch (start us, length us, event | category | flops | bytes accessed | tf_op | source)
XLA Modules:
  0.0 84.3 jit_solution(691979146856504602)
XLA Ops:
  0.0 0.0 copy-start.1
  0.0 4.4 %all-to-all-start = ((bf16[4,8,16,128]{3,0,2,1:T(4,128)(2,1)}), bf16[4,8,16,128]{3,0,2,1:T(4,128)(2,1)S(1)}, u32[]{:S(2)}, u32[]{:S(2)}) async-start(bf16[4,8,16,128]{3,0,2,1:T(4,128)(2,1)} %bitcast.22), calls=%async_computation | async-start | bytes 262144 | tf_op jit(solution)/shard_map/all_to_all | solution.py:77
  4.4 0.0 copy-start.2
  4.4 0.0 copy-start.3
  4.5 0.0 copy-start.4
  4.5 0.0 copy-done.1
  4.5 0.6 copy-done.2
  5.1 0.0 copy-done.3
  5.1 0.0 copy-done.4
  5.1 0.8 tables.1
  5.9 4.6 %all-to-all-done = bf16[4,8,16,128]{3,0,2,1:T(4,128)(2,1)S(1)} async-done(((bf16[4,8,16,128]{3,0,2,1:T(4,128)(2,1)}), bf16[4,8,16,128]{3,0,2,1:T(4,128)(2,1)S(1)}, u32[]{:S(2)}, u32[]{:S(2)}) %all-to-all-start) | async-done | bytes 131104 | tf_op jit(solution)/shard_map/all_to_all | solution.py:77
  10.5 0.3 mix.1
  10.8 8.5 %all_to_all.15 = bf16[8,64,128]{2,1,0:T(8,128)(2,1)S(1)} all-to-all(bf16[8,64,128]{2,1,0:T(8,128)(2,1)S(1)} %bitcast.17), channel_id=1, replica_groups=mesh['shell'=8,'tile'=128] {'shell'}, dimensions={0} | all-to-all | bytes 262144 | tf_op jit(solution)/shard_map/all_to_all | solution.py:79
  19.3 0.0 copy-start
  19.3 63.7 %all_to_all.16 = bf16[128,4,128]{2,1,0:T(4,128)(2,1)S(1)} all-to-all(bf16[128,4,128]{2,1,0:T(4,128)(2,1)S(1)} %bitcast.21), channel_id=1, replica_groups=mesh['shell'=8,'tile'=128] {'tile'}, dimensions={0} | all-to-all | bytes 262144 | tf_op jit(solution)/shard_map/all_to_all | solution.py:80
  83.0 0.0 copy-done
  83.0 1.3 %smooth.1 = bf16[512,128]{1,0:T(8,128)(2,1)} custom-call(bf16[512,512]{1,0:T(8,128)(2,1)S(1)} %get-tuple-element.7.smooth_ref, bf16[128,128]{1,0:T(8,128)(2,1)S(1)} %copy-done, bf16[512,128]{1,0:T(8,128)(2,1)S(1)} %bitcast.15), custom_call_target="tpu_custom_call" | custom-call | tf_op jit(solution)/shard_map/smooth/pallas_call | solution.py:81
Async XLA Ops:
  0.0 4.5 %copy-start.1 = (bf16[128,128]{1,0:T(8,128)(2,1)S(1)}, bf16[128,128]{1,0:T(8,128)(2,1)}, u32[]{:S(2)}) copy-start(bf16[128,128]{1,0:T(8,128)(2,1)} %refs_3_.1) | copy-start | bytes 98308
  0.0 10.5 %all-to-all-start = ((bf16[4,8,16,128]{3,0,2,1:T(4,128)(2,1)}), bf16[4,8,16,128]{3,0,2,1:T(4,128)(2,1)S(1)}, u32[]{:S(2)}, u32[]{:S(2)}) async-start(bf16[4,8,16,128]{3,0,2,1:T(4,128)(2,1)} %bitcast.22), calls=%async_computation | async-start | bytes 262144 | tf_op jit(solution)/shard_map/all_to_all | solution.py:77
  4.4 0.7 copy-start.2
  4.4 0.7 copy-start.3
  4.5 0.7 copy-start.4
  19.3 63.7 %copy-start = (bf16[128,128]{1,0:T(8,128)(2,1)S(1)}, bf16[128,128]{1,0:T(8,128)(2,1)}, u32[]{:S(2)}) copy-start(bf16[128,128]{1,0:T(8,128)(2,1)} %cols_ref.1) | copy-start | bytes 98308

commit v2 on v1

--- a/solution.py
+++ b/solution.py
@@ -14,7 +14,7 @@
     return lax.broadcasted_iota(jnp.int32, shape, axis)
 
 
-def tables_kernel(groups, band_ref, weight_ref, ray_ref, rows_ref, mix_ref, smooth_ref):
+def tables_kernel(groups, ys, band_ref, weight_ref, ray_ref, rows_ref, mix_ref, smooth_ref):
     count = band_ref.shape[1]
     per = count // groups
     band = count // 2
@@ -30,12 +30,15 @@
     values = 8.0 * weight * chi_shell * (chi_source - chi_shell) / chi_source
     inside = (shell >= low) & (shell < low + band)
     table = jnp.where(inside, values, 0.0).astype(jnp.bfloat16)
-    spot = iota((size, count), 0)
-    pick = (iota((size, count), 1) == spot // run * per + spot % per).astype(jnp.bfloat16)
-    by_shell = jnp.dot(pick, table, preferred_element_type=jnp.float32).astype(jnp.bfloat16)
-    full = lax.dot_general(by_shell, pick, ROW_BY_ROW, preferred_element_type=jnp.float32)
+    spot, which = iota((size, count), 0), iota((size, count), 1)
+    part = run // ys
+    pick_out = (which == spot // part % groups * per + spot % per).astype(jnp.bfloat16)
+    pick_in = (which == spot // run * per + spot % per).astype(jnp.bfloat16)
+    by_shell = jnp.dot(pick_out, table, preferred_element_type=jnp.float32).astype(jnp.bfloat16)
+    full = lax.dot_general(by_shell, pick_in, ROW_BY_ROW, preferred_element_type=jnp.float32)
     here, there = iota((size, size), 0), iota((size, size), 1)
-    mix_ref[...] = jnp.where(here % run // per == there % run // per, full, 0.0).astype(jnp.bfloat16)
+    tile_out = here % part // per * ys + here // (part * groups)
+    mix_ref[...] = jnp.where(tile_out == there % run // per, full, 0.0).astype(jnp.bfloat16)
 
     side = rows_ref.shape[0]
     each = smooth_ref.shape[0] // side
@@ -63,26 +66,28 @@
 def shards(residual, tile_ray, filter_rows, filter_cols, band_lo, shell_weight):
     planes, rays = residual.shape
     groups = lax.axis_size("shell")
-    ntile = lax.axis_size("tile")
+    zs, ys = lax.axis_size("z"), lax.axis_size("y")
+    ntile = zs * ys
     run = rays // ntile
     lines = planes * ntile
     square = jax.ShapeDtypeStruct((lines, lines), jnp.bfloat16)
     slab = jax.ShapeDtypeStruct((lines, run), jnp.bfloat16)
 
     mix, smooth = pl.pallas_call(
-        lambda *refs: tables_kernel(groups, *refs), out_shape=(square, square), in_specs=[VMEM] * 4, out_specs=(VMEM, VMEM), compiler_params=TRIM, name="tables"
+        lambda *refs: tables_kernel(groups, ys, *refs), out_shape=(square, square), in_specs=[VMEM] * 4, out_specs=(VMEM, VMEM), compiler_params=TRIM, name="tables"
     )(band_lo.reshape(1, -1), shell_weight.reshape(1, -1), tile_ray.reshape(1, -1), filter_rows)
 
     by_tile = residual.reshape(planes, groups, ntile // groups, run)
     spread = lax.all_to_all(by_tile, "shell", 1, 1, tiled=True).transpose(1, 2, 0, 3).reshape(lines, run)
     mixed = pl.pallas_call(mix_kernel, out_shape=slab, in_specs=[VMEM] * 2, out_specs=VMEM, compiler_params=TRIM, name="mix")(mix, spread)
-    own = lax.all_to_all(mixed.reshape(groups, lines // groups, run), "shell", 0, 0, tiled=True)
-    pixels = lax.all_to_all(own.reshape(ntile, planes, run), "tile", 0, 0, tiled=True)
+    own = lax.all_to_all(mixed.reshape(ys * groups, -1, run), ("y", "shell"), 0, 0, tiled=True)
+    pixels = lax.all_to_all(own.reshape(ys, zs, planes, run), "z", 1, 1, tiled=True).transpose(1, 0, 2, 3)
     whole = pl.pallas_call(smooth_kernel, out_shape=slab, in_specs=[VMEM] * 3, out_specs=VMEM, compiler_params=TRIM, name="smooth")(smooth, filter_cols, pixels.reshape(lines, run))
     return whole.reshape(ntile, planes, run).transpose(1, 0, 2).reshape(planes, rays)
 
 
 def solution(mesh):
-    in_specs = (P("shell", "tile"), P("tile"), P(), P(), P(), P())
-    out_specs = P("shell", "tile")
+    mesh = jax.sharding.Mesh(mesh.devices.reshape(8, 32, 4), ("shell", "z", "y"))
+    in_specs = (P("shell", ("z", "y")), P(("z", "y")), P(), P(), P(), P())
+    out_specs = P("shell", ("z", "y"))
     return jax.shard_map(shards, mesh=mesh, in_specs=in_specs, out_specs=out_specs, check_vma=False)

time: 84.7 us -> 85 us (level)
  the two profiles are of different devices: /device:TPU:32 before, /device:TPU:1 now
where the time goes in v2:
time: 85 us; the launch traced here: 84.4 us
  blocking collectives  59.9 us (70%)
  starting transfers between devices  17.5 us (21%)
  waiting for transfers between devices  3.78 us (4%)
  Pallas kernels  2.38 us (3%)
    all_to_all x1, blocking collectives, shards(): lax.all_to_all(own.reshape(ys, zs, planes, run), 'z', 1, 1, tiled=True)  48.7 us
    all_to_all x1, starting transfers between devices, shards(): lax.all_to_all(by_tile, 'shell', 1, 1, tiled=True).transpose(1, 2, 0, 3)  17.5 us
    all_to_all x1, blocking collectives, shards(): lax.all_to_all(mixed.reshape(ys * groups, -1, run), ('y', 'shell'), 0, 0,...  11.2 us
    all_to_all x1, waiting for transfers between devices, shards(): lax.all_to_all(by_tile, 'shell', 1, 1, tiled=True).transpose(1, 2, 0, 3)  3.78 us
  transfers between devices with their start and end apart: 1, of which 1 were waited for; matrix products, arithmetic and copies ran while one was open for 0% of the time, Pallas kernels for 1%

profile of v2, /device:TPU:1, one launch (start us, length us, event | category | flops | bytes accessed | tf_op | source)
XLA Modules:
  0.0 84.4 jit_solution(18397380423952176173)
XLA Ops:
  0.0 0.0 copy-start.1
  0.0 17.5 %all-to-all-start = ((bf16[4,8,16,128]{3,0,2,1:T(4,128)(2,1)}), bf16[4,8,16,128]{3,0,2,1:T(4,128)(2,1)S(1)}, u32[]{:S(2)}, u32[]{:S(2)}) async-start(bf16[4,8,16,128]{3,0,2,1:T(4,128)(2,1)} %bitcast.24), calls=%async_computation | async-start | bytes 262144 | tf_op jit(solution)/shard_map/all_to_all | solution.py:81
  17.5 0.0 copy-start.2
  17.5 0.0 copy-start.3
  17.5 0.0 copy-start.4
  17.5 0.0 copy-done.1
  17.5 0.6 copy-done.2
  18.2 0.0 copy-done.3
  18.2 0.0 copy-done.4
  18.2 0.8 tables.1
  19.0 3.8 %all-to-all-done = bf16[4,8,16,128]{3,0,2,1:T(4,128)(2,1)S(1)} async-done(((bf16[4,8,16,128]{3,0,2,1:T(4,128)(2,1)}), bf16[4,8,16,128]{3,0,2,1:T(4,128)(2,1)S(1)}, u32[]{:S(2)}, u32[]{:S(2)}) %all-to-all-start) | async-done | bytes 131104 | tf_op jit(solution)/shard_map/all_to_all | solution.py:81
  22.8 0.3 mix.1
  23.1 11.2 %all_to_all.15 = bf16[32,16,128]{2,1,0:T(8,128)(2,1)S(1)} all-to-all(bf16[32,16,128]{2,1,0:T(8,128)(2,1)S(1)} %bitcast.19), channel_id=1, replica_groups=mesh['shell'=8,'z'=32,'y'=4] {'y','shell'}, dimensions={0} | all-to-all | bytes 262144 | tf_op jit(solution)/shard_map/all_to_all | solution.py:83
  34.3 0.0 copy-start
  34.4 48.7 %all_to_all.16 = bf16[4,32,4,128]{3,2,0,1:T(4,128)(2,1)S(1)} all-to-all(bf16[4,32,4,128]{3,2,0,1:T(4,128)(2,1)S(1)} %copy.13), channel_id=1, replica_groups=mesh['shell'=8,'z'=32,'y'=4] {'z'}, dimensions={1} | all-to-all | bytes 262144 | tf_op jit(solution)/shard_map/all_to_all | solution.py:84
  83.1 0.0 copy-done
  83.1 1.3 %smooth.1 = bf16[512,128]{1,0:T(8,128)(2,1)} custom-call(bf16[512,512]{1,0:T(8,128)(2,1)S(1)} %get-tuple-element.7.smooth_ref, bf16[128,128]{1,0:T(8,128)(2,1)S(1)} %copy-done, bf16[512,128]{1,0:T(8,128)(2,1)S(1)} %bitcast.17), custom_call_target="tpu_custom_call" | custom-call | tf_op jit(solution)/shard_map/smooth/pallas_call | solution.py:85
  (1 shorter events, 0.0 us)
Async XLA Ops:
  0.0 17.5 %copy-start.1 = (bf16[128,128]{1,0:T(8,128)(2,1)S(1)}, bf16[128,128]{1,0:T(8,128)(2,1)}, u32[]{:S(2)}) copy-start(bf16[128,128]{1,0:T(8,128)(2,1)} %refs_3_.1) | copy-start | bytes 98308
  0.0 22.8 %all-to-all-start = ((bf16[4,8,16,128]{3,0,2,1:T(4,128)(2,1)}), bf16[4,8,16,128]{3,0,2,1:T(4,128)(2,1)S(1)}, u32[]{:S(2)}, u32[]{:S(2)}) async-start(bf16[4,8,16,128]{3,0,2,1:T(4,128)(2,1)} %bitcast.24), calls=%async_computation | async-start | bytes 262144 | tf_op jit(solution)/shard_map/all_to_all | solution.py:81
  17.5 0.7 copy-start.2
  17.5 0.7 copy-start.3
  17.5 0.7 copy-start.4
  34.3 48.8 %copy-start = (bf16[128,128]{1,0:T(8,128)(2,1)S(1)}, bf16[128,128]{1,0:T(8,128)(2,1)}, u32[]{:S(2)}) copy-start(bf16[128,128]{1,0:T(8,128)(2,1)} %cols_ref.1) | copy-start | bytes 98308

commit v3 on v1

v3 whole, which is shorter than its diff:
```python
import jax
import jax.numpy as jnp
from jax import lax
from jax.experimental import pallas as pl
from jax.experimental.pallas import tpu as pltpu
from jax.sharding import Mesh, PartitionSpec as P

VMEM = pl.BlockSpec(memory_space=pltpu.VMEM)
TRIM = pltpu.CompilerParams(vmem_limit_bytes=16 * 2**20)
ROW_BY_ROW = (((1,), (1,)), ((), ()))
BF16 = jnp.bfloat16
F32 = jnp.float32

X, CORE, Z, Y = 4, 2, 32, 4
SHELL = X * CORE
SIDE = 128
PER = 4
PART = SIDE // X
ZR = Z // X
LINES = PER * Z * Y


def iota(shape, axis):
    return lax.broadcasted_iota(jnp.int32, shape, axis)


def one_hot(match):
    return match.astype(BF16)


def dot(a, b):
    return jnp.dot(a, b, preferred_element_type=F32)


def tables_kernel(band_ref, weight_ref, ray_ref, rows_ref, cols_ref, mix_ref, smooth_ref, wide_ref):
    count = SHELL * PER
    band = count // 2
    core = lax.axis_index("core")
    shell, plane = iota((count, count), 0), iota((count, count), 1)
    low = jnp.broadcast_to(band_ref[...], (count, count))
    lanes = jnp.broadcast_to(weight_ref[...], (count, count))
    weight = jnp.sum(jnp.where(shell == plane, lanes, 0.0), axis=1, keepdims=True)
    chi_shell = (shell.astype(F32) + 0.5) / count
    chi_source = (low.astype(F32) + band) / count
    values = 8.0 * weight * chi_shell * (chi_source - chi_shell) / chi_source
    inside = (shell >= low) & (shell < low + band)
    table = jnp.where(inside, values, 0.0).astype(BF16)

    spot, which = iota((LINES, count), 0), iota((LINES, count), 1)
    pick_out = one_hot(which == (spot // SIDE * CORE + core) * PER + spot % PER)
    spot, which = iota((CORE * LINES, count), 0), iota((CORE * LINES, count), 1)
    pick_in = one_hot(which == spot // SIDE * PER + spot % PER)
    full = lax.dot_general(dot(pick_out, table).astype(BF16), pick_in, ROW_BY_ROW, preferred_element_type=F32)
    here, there = iota((LINES, CORE * LINES), 0), iota((LINES, CORE * LINES), 1)
    mix_ref[...] = jnp.where(here % SIDE // PER == there % SIDE // PER, full, 0.0).astype(BF16)

    line, lane = iota((LINES, SIDE), 0), iota((LINES, SIDE), 1)
    spread = lax.dot_general(one_hot(lane == line // PER), rows_ref[...], ROW_BY_ROW, preferred_element_type=F32).astype(BF16)
    source = one_hot(ray_ref[...] == line % SIDE // PER * Y + line // SIDE)
    product = lax.dot_general(spread, source, ROW_BY_ROW, preferred_element_type=F32)
    here, there = iota((LINES, LINES), 0), iota((LINES, LINES), 1)
    smooth_ref[...] = jnp.where(here % PER == there % PER, product, 0.0).astype(BF16)

    cols = dot(one_hot(lane == line // SIDE * PART + line % PART), cols_ref[...])
    for y in range(Y):
        wide_ref[:, y * SIDE : (y + 1) * SIDE] = jnp.where(line % SIDE // PART == y, cols, 0.0).astype(BF16)


def swap(slabs):
    return [jnp.concatenate([s[:, k * PART : (k + 1) * PART] for s in slabs], axis=1) for k in range(X)]


def send_kernel(rays_ref, out_ref):
    rays = rays_ref[...]
    wide = jnp.concatenate([rays[k * SIDE : (k + 1) * SIDE] for k in range(X)], axis=1)
    to, at = iota((SIDE, SIDE), 0), iota((SIDE, SIDE), 1)
    run = ZR * PER
    order = one_hot(at == to % run // PER * (Y * PER) + to // run * PER + to % PER)
    turned = dot(order, wide)
    for x, slab in enumerate(swap([turned[:, k * SIDE : (k + 1) * SIDE] for k in range(X)])):
        slab = slab.astype(BF16)
        for core in range(CORE):
            at_row = (x * CORE + core) * SIDE
            out_ref[at_row : at_row + SIDE] = slab


def mix_kernel(mix_ref, planes_ref, out_ref):
    mixed = dot(mix_ref[...], planes_ref[...])
    run = ZR * PER
    for x in range(X):
        rows = [mixed[x * SIDE + y * run : x * SIDE + (y + 1) * run] for y in range(Y)]
        for k, slab in enumerate(swap(rows)):
            at_row = x * SIDE + k * run
            out_ref[at_row : at_row + run] = slab.astype(BF16)


def smooth_kernel(smooth_ref, wide_ref, pixels_ref, out_ref):
    pixels = pixels_ref[...]
    flat = jnp.concatenate([pixels[x * SIDE : (x + 1) * SIDE] for x in range(X)], axis=1)
    half = dot(flat, wide_ref[...])
    half = jnp.concatenate([half[:, y * SIDE : (y + 1) * SIDE] for y in range(Y)], axis=0)
    upper = half.astype(BF16)
    lower = (half - upper.astype(F32)).astype(BF16)
    out_ref[...] = (dot(smooth_ref[...], upper) + dot(smooth_ref[...], lower)).astype(BF16)


def call(kernel, name, shapes, *args):
    outs = [jax.ShapeDtypeStruct(shape, BF16) for shape in shapes]
    specs = {"in_specs": [VMEM] * len(args), "out_specs": [VMEM] * len(shapes)}
    return pl.pallas_call(kernel, out_shape=outs, compiler_params=TRIM, name=name, **specs)(*args)


def shards(residual, tile_ray, filter_rows, filter_cols, band_lo, shell_weight):
    tiles = Z * Y
    mix, smooth, wide = call(
        tables_kernel, "tables", [(LINES, CORE * LINES), (LINES, LINES), (LINES, LINES)],
        band_lo.reshape(1, -1), shell_weight.reshape(1, -1), tile_ray.reshape(1, -1), filter_rows, filter_cols,
    )
    rays = residual.reshape(PER, tiles, SIDE).transpose(1, 0, 2).reshape(LINES, SIDE)
    (send,) = call(send_kernel, "send", [(CORE * LINES, SIDE)], rays)
    peers = SHELL * Y
    planes = lax.all_to_all(send.reshape(peers, -1, SIDE), ("x", "core", "y"), 0, 0, tiled=True)
    (mixed,) = call(mix_kernel, "mix", [(LINES, SIDE)], mix, planes.reshape(CORE * LINES, SIDE))
    pixels = lax.all_to_all(mixed.reshape(X * Z, PER, SIDE), ("x", "z"), 0, 0, tiled=True)
    (whole,) = call(smooth_kernel, "smooth", [(LINES, SIDE)], smooth, wide, pixels.reshape(LINES, SIDE))
    return whole.reshape(tiles, PER, SIDE).transpose(1, 0, 2).reshape(PER, tiles * SIDE)


def solution(mesh):
    mesh = Mesh(mesh.devices.reshape(X, CORE, Z, Y), ("x", "core", "z", "y"))
    slab = P(("x", "core"), ("z", "y"))
    in_specs = (slab, P(("z", "y")), P(), P(), P(), P())
    return jax.shard_map(shards, mesh=mesh, in_specs=in_specs, out_specs=slab, check_vma=False)
```

time: 84.7 us -> 83.4 us (0.985)
  the two profiles are of different devices: /device:TPU:32 before, /device:TPU:1 now
where the time goes in v3:
time: 83.4 us; the launch traced here: 82.7 us
  blocking collectives  52.3 us (63%)
  starting transfers between devices  17.8 us (21%)
  waiting for transfers between devices  7.22 us (9%)
  Pallas kernels  3.81 us (5%)
  local copies, waits for them, and re-layouts  1.56 us (2%)
    all_to_all x1, blocking collectives, shards(): lax.all_to_all(mixed.reshape(X * Z, PER, SIDE), ('x', 'z'), 0, 0, tiled=T...  52.3 us
    all_to_all x1, starting transfers between devices, shards(): lax.all_to_all(send.reshape(peers, -1, SIDE), ('x', 'core', 'y'), 0, 0, t...  17.8 us
    all_to_all x1, waiting for transfers between devices, shards(): lax.all_to_all(send.reshape(peers, -1, SIDE), ('x', 'core', 'y'), 0, 0, t...  7.22 us
    pallas_call x4, Pallas kernels, call(): pl.pallas_call(kernel, out_shape=outs, compiler_params=TRIM, name=name, *...  3.81 us
  transfers between devices with their start and end apart: 1, of which 1 were waited for; matrix products, arithmetic and copies ran while one was open for 0% of the time, Pallas kernels for 1%

profile of v3, /device:TPU:1, one launch (start us, length us, event | category | flops | bytes accessed | tf_op | source)
XLA Modules:
  0.0 82.7 jit_solution(5584913402118480558)
XLA Ops:
  0.0 0.0 copy-start
  0.0 0.9 %copy-done = bf16[4,16384]{1,0:T(4,128)(2,1)S(1)} copy-done((bf16[4,16384]{1,0:T(4,128)(2,1)S(1)}, bf16[4,16384]{1,0:T(4,128)(2,1)}, u32[]{:S(2)}) %copy-start) | copy-done | bytes 131096
  0.9 1.0 %send.1 = bf16[1024,128]{1,0:T(8,128)(2,1)} custom-call(bf16[512,128]{1,0:T(8,128)(2,1)S(1)} %bitcast.20), custom_call_target="tpu_custom_call" | custom-call | tf_op jit(solution)/shard_map/send/pallas_call | solution.py:110
  1.9 0.0 copy-start.1
  1.9 0.0 copy-start.2
  1.9 17.8 %all-to-all-start = ((bf16[32,32,128]{2,1,0:T(8,128)(2,1)}), bf16[32,32,128]{2,1,0:T(8,128)(2,1)S(1)}, u32[]{:S(2)}, u32[]{:S(2)}) async-start(bf16[32,32,128]{2,1,0:T(8,128)(2,1)} %bitcast.6), calls=%async_computation | async-start | bytes 524288 | tf_op jit(solution)/shard_map/all_to_all | solution.py:122
  19.7 0.0 copy-start.3
  19.7 0.0 copy-start.4
  19.7 0.0 copy-start.5
  19.8 0.0 copy-done.1
  19.8 0.0 copy-done.2
  19.8 0.6 copy-done.3
  20.4 0.0 copy-done.4
  20.4 0.0 copy-done.5
  20.4 1.0 %tables.1 = (bf16[512,1024]{1,0:T(8,128)(2,1)S(1)}, bf16[512,512]{1,0:T(8,128)(2,1)S(1)}, bf16[512,512]{1,0:T(8,128)(2,1)S(1)}) custom-call(s32[1,32]{1,0:T(1,128)S(1)} %bitcast.21, f32[1,32]{1,0:T(1,128)S(1)} %bitcast.22, s32[1,128]{1,0:T(1,128)S(1)} %bitcast.23, bf16[128,128]{1,0:T(8,128)(2,1)S(1)} %copy-done.1, bf16[128,128]{1,0:T(8,128)(2,1)S(1)} %copy-done.2), custom_call_target="tpu_custom_call" | custom-call | tf_op jit(solution)/shard_map/tables/pallas_call | solution.py:110
  21.4 7.2 %all-to-all-done = bf16[32,32,128]{2,1,0:T(8,128)(2,1)S(1)} async-done(((bf16[32,32,128]{2,1,0:T(8,128)(2,1)}), bf16[32,32,128]{2,1,0:T(8,128)(2,1)S(1)}, u32[]{:S(2)}, u32[]{:S(2)}) %all-to-all-start) | async-done | bytes 262176 | tf_op jit(solution)/shard_map/all_to_all | solution.py:122
  28.6 0.5 mix.1
  29.1 52.3 %all_to_all.10 = bf16[128,4,128]{2,1,0:T(4,128)(2,1)S(1)} all-to-all(bf16[128,4,128]{2,1,0:T(4,128)(2,1)S(1)} %bitcast.19), channel_id=1, replica_groups=mesh['x'=4,'core'=2,'z'=32,'y'=4] {'x','z'}, dimensions={0} | all-to-all | bytes 262144 | tf_op jit(solution)/shard_map/all_to_all | solution.py:124
  81.4 1.3 %smooth.1 = bf16[512,128]{1,0:T(8,128)(2,1)} custom-call(bf16[512,512]{1,0:T(8,128)(2,1)S(1)} %get-tuple-element.8.smooth_ref, bf16[512,512]{1,0:T(8,128)(2,1)S(1)} %get-tuple-element.9.wide_ref, bf16[512,128]{1,0:T(8,128)(2,1)S(1)} %bitcast.18), custom_call_target="tpu_custom_call" | custom-call | tf_op jit(solution)/shard_map/smooth/pallas_call | solution.py:110
Async XLA Ops:
  0.0 0.9 %copy-start = (bf16[4,16384]{1,0:T(4,128)(2,1)S(1)}, bf16[4,16384]{1,0:T(4,128)(2,1)}, u32[]{:S(2)}) copy-start(bf16[4,16384]{1,0:T(4,128)(2,1)} %param.6) | copy-start | bytes 393220
  1.9 17.8 %copy-start.1 = (bf16[128,128]{1,0:T(8,128)(2,1)S(1)}, bf16[128,128]{1,0:T(8,128)(2,1)}, u32[]{:S(2)}) copy-start(bf16[128,128]{1,0:T(8,128)(2,1)} %rows_ref.1) | copy-start | bytes 98308
  1.9 17.8 %copy-start.2 = (bf16[128,128]{1,0:T(8,128)(2,1)S(1)}, bf16[128,128]{1,0:T(8,128)(2,1)}, u32[]{:S(2)}) copy-start(bf16[128,128]{1,0:T(8,128)(2,1)} %cols_ref.1) | copy-start | bytes 98308
  1.9 26.7 %all-to-all-start = ((bf16[32,32,128]{2,1,0:T(8,128)(2,1)}), bf16[32,32,128]{2,1,0:T(8,128)(2,1)S(1)}, u32[]{:S(2)}, u32[]{:S(2)}) async-start(bf16[32,32,128]{2,1,0:T(8,128)(2,1)} %bitcast.6), calls=%async_computation | async-start | bytes 524288 | tf_op jit(solution)/shard_map/all_to_all | solution.py:122
  19.7 0.7 copy-start.3
  19.7 0.7 copy-start.4
  19.7 0.7 copy-start.5

commit v4 on v3

--- a/solution.py
+++ b/solution.py
@@ -18,6 +18,7 @@
 PART = SIDE // X
 ZR = Z // X
 LINES = PER * Z * Y
+FIRST = 17
 
 
 def iota(shape, axis):
@@ -56,7 +57,7 @@
 
     line, lane = iota((LINES, SIDE), 0), iota((LINES, SIDE), 1)
     spread = lax.dot_general(one_hot(lane == line // PER), rows_ref[...], ROW_BY_ROW, preferred_element_type=F32).astype(BF16)
-    source = one_hot(ray_ref[...] == line % SIDE // PER * Y + line // SIDE)
+    source = one_hot(ray_ref[...] == (line % SIDE // PER + FIRST) % Z * Y + line // SIDE)
     product = lax.dot_general(spread, source, ROW_BY_ROW, preferred_element_type=F32)
     here, there = iota((LINES, LINES), 0), iota((LINES, LINES), 1)
     smooth_ref[...] = jnp.where(here % PER == there % PER, product, 0.0).astype(BF16)
@@ -71,7 +72,8 @@
 
 
 def send_kernel(rays_ref, out_ref):
-    rays = rays_ref[...]
+    cut = FIRST * Y * PER
+    rays = jnp.concatenate([rays_ref[cut:], rays_ref[:cut]], axis=0)
     wide = jnp.concatenate([rays[k * SIDE : (k + 1) * SIDE] for k in range(X)], axis=1)
     to, at = iota((SIDE, SIDE), 0), iota((SIDE, SIDE), 1)
     run = ZR * PER
@@ -121,7 +123,10 @@
     peers = SHELL * Y
     planes = lax.all_to_all(send.reshape(peers, -1, SIDE), ("x", "core", "y"), 0, 0, tiled=True)
     (mixed,) = call(mix_kernel, "mix", [(LINES, SIDE)], mix, planes.reshape(CORE * LINES, SIDE))
-    pixels = lax.all_to_all(mixed.reshape(X * Z, PER, SIDE), ("x", "z"), 0, 0, tiled=True)
+    members = [[x * Z + (FIRST + z) % Z for x in range(X) for z in range(Z)]]
+    pixels = lax.all_to_all(
+        mixed.reshape(X * Z, PER, SIDE), ("x", "z"), 0, 0, axis_index_groups=members, tiled=True
+    )
     (whole,) = call(smooth_kernel, "smooth", [(LINES, SIDE)], smooth, wide, pixels.reshape(LINES, SIDE))
     return whole.reshape(tiles, PER, SIDE).transpose(1, 0, 2).reshape(PER, tiles * SIDE)
 

time: 83.4 us -> 72.4 us (0.87)
  blocking collectives: 52.3 us -> 41.6 us
    all_to_all x1, blocking collectives: 52.3 us -> 41.6 us  [shards(): lax.all_to_all(mixed.reshape(X * Z, PER, SIDE), ('x', 'z'), 0, 0, axis_in...]
where the time goes in v4:
time: 72.4 us; the launch traced here: 72.1 us
  blocking collectives  41.6 us (57%)
  starting transfers between devices  17.8 us (25%)
  waiting for transfers between devices  7.14 us (10%)
  Pallas kernels  3.88 us (5%)
  local copies, waits for them, and re-layouts  1.56 us (2%)
    all_to_all x1, blocking collectives, shards(): lax.all_to_all(mixed.reshape(X * Z, PER, SIDE), ('x', 'z'), 0, 0, axis_in...  41.6 us
    all_to_all x1, starting transfers between devices, shards(): lax.all_to_all(send.reshape(peers, -1, SIDE), ('x', 'core', 'y'), 0, 0, t...  17.8 us
    all_to_all x1, waiting for transfers between devices, shards(): lax.all_to_all(send.reshape(peers, -1, SIDE), ('x', 'core', 'y'), 0, 0, t...  7.14 us
    pallas_call x4, Pallas kernels, call(): pl.pallas_call(kernel, out_shape=outs, compiler_params=TRIM, name=name, *...  3.88 us
    unnamed x12, local copies, waits for them, and re-layouts  1.56 us
  transfers between devices with their start and end apart: 1, of which 1 were waited for; matrix products, arithmetic and copies ran while one was open for 0% of the time, Pallas kernels for 1%

profile of v4, /device:TPU:1, one launch (start us, length us, event | category | flops | bytes accessed | tf_op | source)
XLA Modules:
  0.0 72.1 jit_solution(8821128439127772603)
XLA Ops:
  0.0 0.0 copy-start
  0.0 0.9 %copy-done = bf16[4,16384]{1,0:T(4,128)(2,1)S(1)} copy-done((bf16[4,16384]{1,0:T(4,128)(2,1)S(1)}, bf16[4,16384]{1,0:T(4,128)(2,1)}, u32[]{:S(2)}) %copy-start) | copy-done | bytes 131096
  0.9 1.0 %send.1 = bf16[1024,128]{1,0:T(8,128)(2,1)} custom-call(bf16[512,128]{1,0:T(8,128)(2,1)S(1)} %bitcast.20), custom_call_target="tpu_custom_call" | custom-call | tf_op jit(solution)/shard_map/send/pallas_call | solution.py:112
  1.9 0.0 copy-start.1
  1.9 0.0 copy-start.2
  1.9 17.8 %all-to-all-start = ((bf16[32,32,128]{2,1,0:T(8,128)(2,1)}), bf16[32,32,128]{2,1,0:T(8,128)(2,1)S(1)}, u32[]{:S(2)}, u32[]{:S(2)}) async-start(bf16[32,32,128]{2,1,0:T(8,128)(2,1)} %bitcast.6), calls=%async_computation | async-start | bytes 524288 | tf_op jit(solution)/shard_map/all_to_all | solution.py:124
  19.7 0.0 copy-start.3
  19.7 0.0 copy-start.4
  19.7 0.0 copy-start.5
  19.8 0.0 copy-done.1
  19.8 0.0 copy-done.2
  19.8 0.6 copy-done.3
  20.4 0.0 copy-done.4
  20.4 0.0 copy-done.5
  20.4 1.0 %tables.1 = (bf16[512,1024]{1,0:T(8,128)(2,1)S(1)}, bf16[512,512]{1,0:T(8,128)(2,1)S(1)}, bf16[512,512]{1,0:T(8,128)(2,1)S(1)}) custom-call(s32[1,32]{1,0:T(1,128)S(1)} %bitcast.21, f32[1,32]{1,0:T(1,128)S(1)} %bitcast.22, s32[1,128]{1,0:T(1,128)S(1)} %bitcast.23, bf16[128,128]{1,0:T(8,128)(2,1)S(1)} %copy-done.1, bf16[128,128]{1,0:T(8,128)(2,1)S(1)} %copy-done.2), custom_call_target="tpu_custom_call" | custom-call | tf_op jit(solution)/shard_map/tables/pallas_call | solution.py:112
  21.5 7.1 %all-to-all-done = bf16[32,32,128]{2,1,0:T(8,128)(2,1)S(1)} async-done(((bf16[32,32,128]{2,1,0:T(8,128)(2,1)}), bf16[32,32,128]{2,1,0:T(8,128)(2,1)S(1)}, u32[]{:S(2)}, u32[]{:S(2)}) %all-to-all-start) | async-done | bytes 262176 | tf_op jit(solution)/shard_map/all_to_all | solution.py:124
  28.6 0.5 mix.1
  29.1 41.6 %all_to_all.10 = bf16[128,4,128]{2,1,0:T(4,128)(2,1)S(1)} all-to-all(bf16[128,4,128]{2,1,0:T(4,128)(2,1)S(1)} %bitcast.19), channel_id=1, replica_groups={{68,72,76,80,84,88,92,96,100,104,108,112,116,120,124,0,4,8,12,16,20,24,..., dimensions={0} | all-to-all | bytes 262144 | tf_op jit(solution)/shard_map/all_to_all | solution.py:127
  70.8 1.3 %smooth.1 = bf16[512,128]{1,0:T(8,128)(2,1)} custom-call(bf16[512,512]{1,0:T(8,128)(2,1)S(1)} %get-tuple-element.8.smooth_ref, bf16[512,512]{1,0:T(8,128)(2,1)S(1)} %get-tuple-element.9.wide_ref, bf16[512,128]{1,0:T(8,128)(2,1)S(1)} %bitcast.18), custom_call_target="tpu_custom_call" | custom-call | tf_op jit(solution)/shard_map/smooth/pallas_call | solution.py:112
Async XLA Ops:
  0.0 0.9 %copy-start = (bf16[4,16384]{1,0:T(4,128)(2,1)S(1)}, bf16[4,16384]{1,0:T(4,128)(2,1)}, u32[]{:S(2)}) copy-start(bf16[4,16384]{1,0:T(4,128)(2,1)} %param.6) | copy-start | bytes 393220
  1.9 17.8 %copy-start.1 = (bf16[128,128]{1,0:T(8,128)(2,1)S(1)}, bf16[128,128]{1,0:T(8,128)(2,1)}, u32[]{:S(2)}) copy-start(bf16[128,128]{1,0:T(8,128)(2,1)} %rows_ref.1) | copy-start | bytes 98308
  1.9 17.8 %copy-start.2 = (bf16[128,128]{1,0:T(8,128)(2,1)S(1)}, bf16[128,128]{1,0:T(8,128)(2,1)}, u32[]{:S(2)}) copy-start(bf16[128,128]{1,0:T(8,128)(2,1)} %cols_ref.1) | copy-start | bytes 98308
  1.9 26.7 %all-to-all-start = ((bf16[32,32,128]{2,1,0:T(8,128)(2,1)}), bf16[32,32,128]{2,1,0:T(8,128)(2,1)S(1)}, u32[]{:S(2)}, u32[]{:S(2)}) async-start(bf16[32,32,128]{2,1,0:T(8,128)(2,1)} %bitcast.6), calls=%async_computation | async-start | bytes 524288 | tf_op jit(solution)/shard_map/all_to_all | solution.py:124
  19.7 0.7 copy-start.3
  19.7 0.7 copy-start.4
  19.7 0.7 copy-start.5

commit v5 on v3

v5 whole, which is shorter than its diff:
```python
import jax
import jax.numpy as jnp
from jax import lax
from jax.experimental import pallas as pl
from jax.experimental.pallas import tpu as pltpu
from jax.sharding import Mesh, PartitionSpec as P

VMEM = pl.BlockSpec(memory_space=pltpu.VMEM)
HBM = pl.BlockSpec(memory_space=pltpu.HBM)
TRIM = pltpu.CompilerParams(vmem_limit_bytes=16 * 2**20)
ROW_BY_ROW = (((1,), (1,)), ((), ()))
BF16 = jnp.bfloat16
F32 = jnp.float32

X, CORE, Z, Y = 4, 2, 32, 4
SHELL = X * CORE
SIDE = 128
PER = 4
PART = SIDE // X
ZR = Z // X
LINES = PER * Z * Y
X0, Y0, Z0 = 2, 2, 17


SLAB = pltpu.VMEM((LINES, SIDE), BF16)


def dmas(count):
    return pltpu.SemaphoreType.DMA((count,))


def iota(shape, axis):
    return lax.broadcasted_iota(jnp.int32, shape, axis)


def one_hot(match):
    return match.astype(BF16)


def dot(a, b):
    return jnp.dot(a, b, preferred_element_type=F32)


def tables_kernel(band_ref, weight_ref, ray_ref, rows_ref, cols_ref, mix_ref, smooth_ref, wide_ref):
    count = SHELL * PER
    band = count // 2
    core = lax.axis_index("core")
    shell, plane = iota((count, count), 0), iota((count, count), 1)
    low = jnp.broadcast_to(band_ref[...], (count, count))
    lanes = jnp.broadcast_to(weight_ref[...], (count, count))
    weight = jnp.sum(jnp.where(shell == plane, lanes, 0.0), axis=1, keepdims=True)
    chi_shell = (shell.astype(F32) + 0.5) / count
    chi_source = (low.astype(F32) + band) / count
    values = 8.0 * weight * chi_shell * (chi_source - chi_shell) / chi_source
    inside = (shell >= low) & (shell < low + band)
    table = jnp.where(inside, values, 0.0).astype(BF16)

    spot, which = iota((LINES, count), 0), iota((LINES, count), 1)
    pick_out = one_hot(which == ((spot // SIDE + X0) % X * CORE + core) * PER + spot % PER)
    spot, which = iota((CORE * LINES, count), 0), iota((CORE * LINES, count), 1)
    source = (spot // (CORE * SIDE) + X0) % X * CORE + spot // SIDE % CORE
    pick_in = one_hot(which == source * PER + spot % PER)
    full = lax.dot_general(dot(pick_out, table).astype(BF16), pick_in, ROW_BY_ROW, preferred_element_type=F32)
    here, there = iota((LINES, CORE * LINES), 0), iota((LINES, CORE * LINES), 1)
    mix_ref[...] = jnp.where(here % SIDE // PER == there % SIDE // PER, full, 0.0).astype(BF16)

    line, lane = iota((LINES, SIDE), 0), iota((LINES, SIDE), 1)
    spread = lax.dot_general(one_hot(lane == line // PER), rows_ref[...], ROW_BY_ROW, preferred_element_type=F32).astype(BF16)
    block = (line % SIDE // PER + Z0) % Z * Y + (line // SIDE + Y0) % Y
    product = lax.dot_general(spread, one_hot(ray_ref[...] == block), ROW_BY_ROW, preferred_element_type=F32)
    here, there = iota((LINES, LINES), 0), iota((LINES, LINES), 1)
    smooth_ref[...] = jnp.where(here % PER == there % PER, product, 0.0).astype(BF16)

    cols = dot(one_hot(lane == (line // SIDE + X0) % X * PART + line % PART), cols_ref[...])
    for y in range(Y):
        wide_ref[:, y * SIDE : (y + 1) * SIDE] = jnp.where(line % SIDE // PART == y, cols, 0.0).astype(BF16)


def swap(slabs):
    return [jnp.concatenate([s[:, k * PART : (k + 1) * PART] for s in slabs], axis=1) for k in range(X)]


def send_kernel(rays_ref, out_ref, rays, slabs, arrived, left):
    cut = Z0 * Y * PER
    pieces = ((cut, 0, LINES - cut), (0, LINES - cut, cut))
    reads = [
        pltpu.make_async_copy(rays_ref.at[pl.ds(start, size)], rays.at[pl.ds(to, size)], arrived.at[k])
        for k, (start, to, size) in enumerate(pieces)
    ]
    for read in reads:
        read.start()
    to, at = iota((SIDE, SIDE), 0), iota((SIDE, SIDE), 1)
    run = ZR * PER
    order = one_hot(at == to % run // PER * (Y * PER) + (to // run + Y0) % Y * PER + to % PER)
    for read in reads:
        read.wait()
    wide = jnp.concatenate([rays[k * SIDE : (k + 1) * SIDE] for k in range(X)], axis=1)
    turned = dot(order, wide)
    parts = swap([turned[:, k * SIDE : (k + 1) * SIDE] for k in range(X)])
    writes = []
    for x in range(X):
        slabs[x * SIDE : (x + 1) * SIDE] = parts[(x + X0) % X].astype(BF16)
        for core in range(CORE):
            k = x * CORE + core
            source = slabs.at[pl.ds(x * SIDE, SIDE)]
            writes.append(pltpu.make_async_copy(source, out_ref.at[pl.ds(k * SIDE, SIDE)], left.at[k]))
            writes[-1].start()
    for write in writes:
        write.wait()


def mix_kernel(mix_ref, planes_ref, out_ref):
    mixed = dot(mix_ref[...], planes_ref[...])
    run = ZR * PER
    for x in range(X):
        rows = [mixed[x * SIDE + y * run : x * SIDE + (y + 1) * run] for y in range(Y)]
        for k, slab in enumerate(swap(rows)):
            at_row = x * SIDE + k * run
            out_ref[at_row : at_row + run] = slab.astype(BF16)


def smooth_kernel(smooth_ref, wide_ref, pixels_ref, out_ref, whole, left):
    pixels = pixels_ref[...]
    flat = jnp.concatenate([pixels[x * SIDE : (x + 1) * SIDE] for x in range(X)], axis=1)
    half = dot(flat, wide_ref[...]).astype(BF16)
    half = jnp.concatenate([half[:, y * SIDE : (y + 1) * SIDE] for y in range(Y)], axis=0)
    part = LINES // 2
    writes = []
    for k in range(2):
        whole[k * part : (k + 1) * part] = dot(smooth_ref[k * part : (k + 1) * part], half).astype(BF16)
        place = pl.ds(k * part, part)
        writes.append(pltpu.make_async_copy(whole.at[place], out_ref.at[place], left.at[k]))
        writes[-1].start()
    for write in writes:
        write.wait()


def call(kernel, name, shapes, *args, ins=VMEM, outs=VMEM, scratch=()):
    out_shape = [jax.ShapeDtypeStruct(shape, BF16) for shape in shapes]
    specs = {"in_specs": [ins] * len(args), "out_specs": [outs] * len(shapes), "scratch_shapes": scratch}
    return pl.pallas_call(kernel, out_shape=out_shape, compiler_params=TRIM, name=name, **specs)(*args)


def shards(residual, tile_ray, filter_rows, filter_cols, band_lo, shell_weight):
    tiles = Z * Y
    mix, smooth, wide = call(
        tables_kernel, "tables", [(LINES, CORE * LINES), (LINES, LINES), (LINES, LINES)],
        band_lo.reshape(1, -1), shell_weight.reshape(1, -1), tile_ray.reshape(1, -1), filter_rows, filter_cols,
    )
    rays = residual.reshape(PER, tiles, SIDE).transpose(1, 0, 2).reshape(LINES, SIDE)
    (send,) = call(
        send_kernel, "send", [(CORE * LINES, SIDE)], rays,
        ins=HBM, outs=HBM, scratch=[SLAB, SLAB, dmas(2), dmas(SHELL)],
    )
    peers = SHELL * Y
    near = [[((X0 + x) % X * CORE + c) * Y + (Y0 + y) % Y for x in range(X) for c in range(CORE) for y in range(Y)]]
    planes = lax.all_to_all(
        send.reshape(peers, -1, SIDE), ("x", "core", "y"), 0, 0, axis_index_groups=near, tiled=True
    )
    (mixed,) = call(mix_kernel, "mix", [(LINES, SIDE)], mix, planes.reshape(CORE * LINES, SIDE))
    far = [[(X0 + x) % X * Z + (Z0 + z) % Z for x in range(X) for z in range(Z)]]
    pixels = lax.all_to_all(
        mixed.reshape(X * Z, PER, SIDE), ("x", "z"), 0, 0, axis_index_groups=far, tiled=True
    )
    (whole,) = call(smooth_kernel, "smooth", [(LINES, SIDE)], smooth, wide, pixels.reshape(LINES, SIDE), outs=HBM, scratch=[SLAB, dmas(2)])
    return whole.reshape(tiles, PER, SIDE).transpose(1, 0, 2).reshape(PER, tiles * SIDE)


def solution(mesh):
    mesh = Mesh(mesh.devices.reshape(X, CORE, Z, Y), ("x", "core", "z", "y"))
    slab = P(("x", "core"), ("z", "y"))
    in_specs = (slab, P(("z", "y")), P(), P(), P(), P())
    return jax.shard_map(shards, mesh=mesh, in_specs=in_specs, out_specs=slab, check_vma=False)
```

time: 83.4 us -> 69.5 us (0.83)
  blocking collectives: 52.3 us -> 39.9 us
  waiting for transfers between devices: 7.22 us -> 2.45 us
  starting transfers between devices: 17.8 us -> 21.1 us
    all_to_all x1, blocking collectives: 52.3 us -> 39.9 us  [shards(): lax.all_to_all(mixed.reshape(X * Z, PER, SIDE), ('x', 'z'), 0, 0, axis_in...]
    all_to_all x1, waiting for transfers between devices: 7.22 us -> 2.45 us  [shards(): lax.all_to_all(send.reshape(peers, -1, SIDE), ('x', 'core', 'y'), 0, 0, a...]
    all_to_all x1, starting transfers between devices: 17.8 us -> 21.1 us  [shards(): lax.all_to_all(send.reshape(peers, -1, SIDE), ('x', 'core', 'y'), 0, 0, a...]
  transfers between devices with their start and end apart: 1 -> 1, of which waited for: 1 -> 1; matrix products, arithmetic and copies ran while one was open for 0% -> 0% of each run, Pallas kernels for 1% -> 2%
where the time goes in v5:
time: 69.5 us; the launch traced here: 69.2 us
  blocking collectives  39.9 us (57%)
  starting transfers between devices  21.1 us (30%)
  Pallas kernels  4.13 us (6%)
  waiting for transfers between devices  2.45 us (4%)
  local copies, waits for them, and re-layouts  1.56 us (2%)
    all_to_all x1, blocking collectives, shards(): lax.all_to_all(mixed.reshape(X * Z, PER, SIDE), ('x', 'z'), 0, 0, axis_in...  39.9 us
    all_to_all x1, starting transfers between devices, shards(): lax.all_to_all(send.reshape(peers, -1, SIDE), ('x', 'core', 'y'), 0, 0, a...  21.1 us
    pallas_call x4, Pallas kernels, call(): pl.pallas_call(kernel, out_shape=out_shape, compiler_params=TRIM, name=na...  4.13 us
    all_to_all x1, waiting for transfers between devices, shards(): lax.all_to_all(send.reshape(peers, -1, SIDE), ('x', 'core', 'y'), 0, 0, a...  2.45 us
    unnamed x12, local copies, waits for them, and re-layouts  1.56 us
  transfers between devices with their start and end apart: 1, of which 1 were waited for; matrix products, arithmetic and copies ran while one was open for 0% of the time, Pallas kernels for 2%

profile of v5, /device:TPU:1, one launch (start us, length us, event | category | flops | bytes accessed | tf_op | source)
XLA Modules:
  0.0 69.2 jit_solution(10348727210652559467)
XLA Ops:
  0.0 0.0 copy-start
  0.0 0.9 %copy-done = bf16[4,16384]{1,0:T(4,128)(2,1)S(1)} copy-done((bf16[4,16384]{1,0:T(4,128)(2,1)S(1)}, bf16[4,16384]{1,0:T(4,128)(2,1)}, u32[]{:S(2)}) %copy-start) | copy-done | bytes 131096
  0.9 1.3 %send.1 = bf16[1024,128]{1,0:T(8,128)(2,1)} custom-call(bf16[512,128]{1,0:T(8,128)(2,1)S(1)} %bitcast.20), custom_call_target="tpu_custom_call" | custom-call | tf_op jit(solution)/shard_map/send/pallas_call | solution.py:141
  2.2 0.0 copy-start.1
  2.2 0.0 copy-start.2
  2.2 21.1 %all-to-all-start = ((bf16[32,32,128]{2,1,0:T(8,128)(2,1)}), bf16[32,32,128]{2,1,0:T(8,128)(2,1)S(1)}, u32[]{:S(2)}, u32[]{:S(2)}) async-start(bf16[32,32,128]{2,1,0:T(8,128)(2,1)} %bitcast.6), calls=%async_computation | async-start | bytes 524288 | tf_op jit(solution)/shard_map/all_to_all | solution.py:157
  23.3 0.0 copy-start.3
  23.4 0.0 copy-start.4
  23.4 0.0 copy-start.5
  23.4 0.0 copy-done.1
  23.4 0.0 copy-done.2
  23.4 0.6 copy-done.3
  24.0 0.0 copy-done.4
  24.0 0.0 copy-done.5
  24.0 1.2 %tables.1 = (bf16[512,1024]{1,0:T(8,128)(2,1)S(1)}, bf16[512,512]{1,0:T(8,128)(2,1)S(1)}, bf16[512,512]{1,0:T(8,128)(2,1)S(1)}) custom-call(s32[1,32]{1,0:T(1,128)S(1)} %bitcast.21, f32[1,32]{1,0:T(1,128)S(1)} %bitcast.22, s32[1,128]{1,0:T(1,128)S(1)} %bitcast.23, bf16[128,128]{1,0:T(8,128)(2,1)S(1)} %copy-done.1, bf16[128,128]{1,0:T(8,128)(2,1)S(1)} %copy-done.2), custom_call_target="tpu_custom_call" | custom-call | tf_op jit(solution)/shard_map/tables/pallas_call | solution.py:141
  25.2 2.5 %all-to-all-done = bf16[32,32,128]{2,1,0:T(8,128)(2,1)S(1)} async-done(((bf16[32,32,128]{2,1,0:T(8,128)(2,1)}), bf16[32,32,128]{2,1,0:T(8,128)(2,1)S(1)}, u32[]{:S(2)}, u32[]{:S(2)}) %all-to-all-start) | async-done | bytes 262176 | tf_op jit(solution)/shard_map/all_to_all | solution.py:157
  27.7 0.5 mix.1
  28.2 39.9 %all_to_all.10 = bf16[128,4,128]{2,1,0:T(4,128)(2,1)S(1)} all-to-all(bf16[128,4,128]{2,1,0:T(4,128)(2,1)S(1)} %bitcast.19), channel_id=1, replica_groups={{580,584,588,592,596,600,604,608,612,616,620,624,628,632,636,512,516,52..., dimensions={0} | all-to-all | bytes 262144 | tf_op jit(solution)/shard_map/all_to_all | solution.py:162
  68.1 1.2 %smooth.1 = bf16[512,128]{1,0:T(8,128)(2,1)} custom-call(bf16[512,512]{1,0:T(8,128)(2,1)S(1)} %get-tuple-element.8.smooth_ref, bf16[512,512]{1,0:T(8,128)(2,1)S(1)} %get-tuple-element.9.wide_ref, bf16[512,128]{1,0:T(8,128)(2,1)S(1)} %bitcast.18), custom_call_target="tpu_custom_call" | custom-call | tf_op jit(solution)/shard_map/smooth/pallas_call | solution.py:141
Async XLA Ops:
  0.0 0.9 %copy-start = (bf16[4,16384]{1,0:T(4,128)(2,1)S(1)}, bf16[4,16384]{1,0:T(4,128)(2,1)}, u32[]{:S(2)}) copy-start(bf16[4,16384]{1,0:T(4,128)(2,1)} %param.6) | copy-start | bytes 393220
  2.2 21.2 %copy-start.1 = (bf16[128,128]{1,0:T(8,128)(2,1)S(1)}, bf16[128,128]{1,0:T(8,128)(2,1)}, u32[]{:S(2)}) copy-start(bf16[128,128]{1,0:T(8,128)(2,1)} %rows_ref.1) | copy-start | bytes 98308
  2.2 21.2 %copy-start.2 = (bf16[128,128]{1,0:T(8,128)(2,1)S(1)}, bf16[128,128]{1,0:T(8,128)(2,1)}, u32[]{:S(2)}) copy-start(bf16[128,128]{1,0:T(8,128)(2,1)} %cols_ref.1) | copy-start | bytes 98308
  2.2 25.5 %all-to-all-start = ((bf16[32,32,128]{2,1,0:T(8,128)(2,1)}), bf16[32,32,128]{2,1,0:T(8,128)(2,1)S(1)}, u32[]{:S(2)}, u32[]{:S(2)}) async-start(bf16[32,32,128]{2,1,0:T(8,128)(2,1)} %bitcast.6), calls=%async_computation | async-start | bytes 524288 | tf_op jit(solution)/shard_map/all_to_all | solution.py:157
  23.3 0.7 copy-start.3
  23.4 0.7 copy-start.4
  23.4 0.7 copy-start.5

commit v6 on v5

--- a/solution.py
+++ b/solution.py
@@ -6,6 +6,7 @@
 from jax.sharding import Mesh, PartitionSpec as P
 
 VMEM = pl.BlockSpec(memory_space=pltpu.VMEM)
+WHOLE = pltpu.CompilerParams(vmem_limit_bytes=60 * 2**20)
 HBM = pl.BlockSpec(memory_space=pltpu.HBM)
 TRIM = pltpu.CompilerParams(vmem_limit_bytes=16 * 2**20)
 ROW_BY_ROW = (((1,), (1,)), ((), ()))
@@ -55,14 +56,15 @@
     inside = (shell >= low) & (shell < low + band)
     table = jnp.where(inside, values, 0.0).astype(BF16)
 
-    spot, which = iota((LINES, count), 0), iota((LINES, count), 1)
-    pick_out = one_hot(which == ((spot // SIDE + X0) % X * CORE + core) * PER + spot % PER)
-    spot, which = iota((CORE * LINES, count), 0), iota((CORE * LINES, count), 1)
-    source = (spot // (CORE * SIDE) + X0) % X * CORE + spot // SIDE % CORE
+    part = ZR * PER
+    spot, which = iota((X * part, count), 0), iota((X * part, count), 1)
+    pick_out = one_hot(which == ((spot // part + X0) % X * CORE + core) * PER + spot % PER)
+    spot, which = iota((SHELL * part, count), 0), iota((SHELL * part, count), 1)
+    source = (spot // (CORE * part) + X0) % X * CORE + spot // part % CORE
     pick_in = one_hot(which == source * PER + spot % PER)
     full = lax.dot_general(dot(pick_out, table).astype(BF16), pick_in, ROW_BY_ROW, preferred_element_type=F32)
-    here, there = iota((LINES, CORE * LINES), 0), iota((LINES, CORE * LINES), 1)
-    mix_ref[...] = jnp.where(here % SIDE // PER == there % SIDE // PER, full, 0.0).astype(BF16)
+    here, there = iota(full.shape, 0), iota(full.shape, 1)
+    mix_ref[...] = jnp.where(here % part // PER == there % part // PER, full, 0.0).astype(BF16)
 
     line, lane = iota((LINES, SIDE), 0), iota((LINES, SIDE), 1)
     spread = lax.dot_general(one_hot(lane == line // PER), rows_ref[...], ROW_BY_ROW, preferred_element_type=F32).astype(BF16)
@@ -110,13 +112,17 @@
 
 
 def mix_kernel(mix_ref, planes_ref, out_ref):
-    mixed = dot(mix_ref[...], planes_ref[...])
-    run = ZR * PER
-    for x in range(X):
-        rows = [mixed[x * SIDE + y * run : x * SIDE + (y + 1) * run] for y in range(Y)]
-        for k, slab in enumerate(swap(rows)):
-            at_row = x * SIDE + k * run
-            out_ref[at_row : at_row + run] = slab.astype(BF16)
+    part = ZR * PER
+    by_y = []
+    for y in range(Y):
+        spots = [g * SIDE + y * part for g in range(SHELL)]
+        by_y.append(jnp.concatenate([planes_ref[spot : spot + part] for spot in spots], axis=0))
+    mixed = dot(mix_ref[...], jnp.concatenate(by_y, axis=1))
+    for k, slab in enumerate(swap([mixed[:, y * SIDE : (y + 1) * SIDE] for y in range(Y)])):
+        slab = slab.astype(BF16)
+        for x in range(X):
+            spot = x * SIDE + k * part
+            out_ref[spot : spot + part] = slab[x * part : (x + 1) * part]
 
 
 def smooth_kernel(smooth_ref, wide_ref, pixels_ref, out_ref, whole, left):
@@ -135,22 +141,22 @@
         write.wait()
 
 
-def call(kernel, name, shapes, *args, ins=VMEM, outs=VMEM, scratch=()):
+def call(kernel, name, shapes, *args, ins=VMEM, outs=VMEM, scratch=(), params=TRIM):
     out_shape = [jax.ShapeDtypeStruct(shape, BF16) for shape in shapes]
     specs = {"in_specs": [ins] * len(args), "out_specs": [outs] * len(shapes), "scratch_shapes": scratch}
-    return pl.pallas_call(kernel, out_shape=out_shape, compiler_params=TRIM, name=name, **specs)(*args)
+    return pl.pallas_call(kernel, out_shape=out_shape, compiler_params=params, name=name, **specs)(*args)
 
 
 def shards(residual, tile_ray, filter_rows, filter_cols, band_lo, shell_weight):
     tiles = Z * Y
     mix, smooth, wide = call(
-        tables_kernel, "tables", [(LINES, CORE * LINES), (LINES, LINES), (LINES, LINES)],
+        tables_kernel, "tables", [(SIDE, 2 * SIDE), (LINES, LINES), (LINES, LINES)],
         band_lo.reshape(1, -1), shell_weight.reshape(1, -1), tile_ray.reshape(1, -1), filter_rows, filter_cols,
     )
     rays = residual.reshape(PER, tiles, SIDE).transpose(1, 0, 2).reshape(LINES, SIDE)
     (send,) = call(
         send_kernel, "send", [(CORE * LINES, SIDE)], rays,
-        ins=HBM, outs=HBM, scratch=[SLAB, SLAB, dmas(2), dmas(SHELL)],
+        ins=HBM, outs=HBM, scratch=[SLAB, SLAB, dmas(2), dmas(SHELL)], params=WHOLE,
     )
     peers = SHELL * Y
     near = [[((X0 + x) % X * CORE + c) * Y + (Y0 + y) % Y for x in range(X) for c in range(CORE) for y in range(Y)]]

time: 69.5 us -> 69.2 us (level)
  local copies, waits for them, and re-layouts: 1.56 us -> 0.66 us
    unnamed x12 -> x10, local copies, waits for them, and re-layouts: 1.56 us -> 0.66 us
  transfers between devices with their start and end apart: 1 -> 1, of which waited for: 1 -> 1; matrix products, arithmetic and copies ran while one was open for 0% -> 0% of each run, Pallas kernels for 2% -> 1%
where the time goes in v6:
time: 69.2 us; the launch traced here: 68.9 us
  blocking collectives  39.9 us (58%)
  starting transfers between devices  21.1 us (30%)
  Pallas kernels  4.24 us (6%)
  waiting for transfers between devices  2.9 us (4%)
    all_to_all x1, blocking collectives, shards(): lax.all_to_all(mixed.reshape(X * Z, PER, SIDE), ('x', 'z'), 0, 0, axis_in...  39.9 us
    all_to_all x1, starting transfers between devices, shards(): lax.all_to_all(send.reshape(peers, -1, SIDE), ('x', 'core', 'y'), 0, 0, a...  21.1 us
    pallas_call x4, Pallas kernels, call(): pl.pallas_call(kernel, out_shape=out_shape, compiler_params=params, name=...  4.24 us
    all_to_all x1, waiting for transfers between devices, shards(): lax.all_to_all(send.reshape(peers, -1, SIDE), ('x', 'core', 'y'), 0, 0, a...  2.9 us
  transfers between devices with their start and end apart: 1, of which 1 were waited for; matrix products, arithmetic and copies ran while one was open for 0% of the time, Pallas kernels for 1%

profile of v6, /device:TPU:1, one launch (start us, length us, event | category | flops | bytes accessed | tf_op | source)
XLA Modules:
  0.0 68.9 jit_solution(9773455938427329560)
XLA Ops:
  0.0 2.0 %send.1 = bf16[1024,128]{1,0:T(8,128)(2,1)} custom-call(bf16[512,128]{1,0:T(8,128)(2,1)} %bitcast.24), custom_call_target="tpu_custom_call" | custom-call | tf_op jit(solution)/shard_map/send/pallas_call | solution.py:147
  2.0 0.0 copy-start
  2.0 0.0 copy-start.1
  2.1 21.1 %all-to-all-start = ((bf16[32,32,128]{2,1,0:T(8,128)(2,1)}), bf16[32,32,128]{2,1,0:T(8,128)(2,1)S(1)}, u32[]{:S(2)}, u32[]{:S(2)}) async-start(bf16[32,32,128]{2,1,0:T(8,128)(2,1)} %bitcast.23), calls=%async_computation | async-start | bytes 524288 | tf_op jit(solution)/shard_map/all_to_all | solution.py:163
  23.2 0.0 copy-start.2
  23.2 0.0 copy-start.3
  23.2 0.0 copy-start.4
  23.2 0.0 copy-done
  23.2 0.0 copy-done.1
  23.2 0.6 copy-done.2
  23.8 0.0 copy-done.3
  23.9 0.0 copy-done.4
  23.9 0.7 %tables.1 = (bf16[128,256]{1,0:T(8,128)(2,1)S(1)}, bf16[512,512]{1,0:T(8,128)(2,1)S(1)}, bf16[512,512]{1,0:T(8,128)(2,1)S(1)}) custom-call(s32[1,32]{1,0:T(1,128)S(1)} %bitcast.20, f32[1,32]{1,0:T(1,128)S(1)} %bitcast.21, s32[1,128]{1,0:T(1,128)S(1)} %bitcast.22, bf16[128,128]{1,0:T(8,128)(2,1)S(1)} %copy-done, bf16[128,128]{1,0:T(8,128)(2,1)S(1)} %copy-done.1), custom_call_target="tpu_custom_call" | custom-call | tf_op jit(solution)/shard_map/tables/pallas_call | solution.py:147
  24.6 2.9 %all-to-all-done = bf16[32,32,128]{2,1,0:T(8,128)(2,1)S(1)} async-done(((bf16[32,32,128]{2,1,0:T(8,128)(2,1)}), bf16[32,32,128]{2,1,0:T(8,128)(2,1)S(1)}, u32[]{:S(2)}, u32[]{:S(2)}) %all-to-all-start) | async-done | bytes 262176 | tf_op jit(solution)/shard_map/all_to_all | solution.py:163
  27.5 0.3 mix.1
  27.9 39.9 %all_to_all.10 = bf16[128,4,128]{2,1,0:T(4,128)(2,1)S(1)} all-to-all(bf16[128,4,128]{2,1,0:T(4,128)(2,1)S(1)} %bitcast.19), channel_id=1, replica_groups={{580,584,588,592,596,600,604,608,612,616,620,624,628,632,636,512,516,52..., dimensions={0} | all-to-all | bytes 262144 | tf_op jit(solution)/shard_map/all_to_all | solution.py:168
  67.7 1.1 %smooth.1 = bf16[512,128]{1,0:T(8,128)(2,1)} custom-call(bf16[512,512]{1,0:T(8,128)(2,1)S(1)} %get-tuple-element.8.smooth_ref, bf16[512,512]{1,0:T(8,128)(2,1)S(1)} %get-tuple-element.9.wide_ref, bf16[512,128]{1,0:T(8,128)(2,1)S(1)} %bitcast.18), custom_call_target="tpu_custom_call" | custom-call | tf_op jit(solution)/shard_map/smooth/pallas_call | solution.py:147
Async XLA Ops:
  2.0 21.2 %copy-start = (bf16[128,128]{1,0:T(8,128)(2,1)S(1)}, bf16[128,128]{1,0:T(8,128)(2,1)}, u32[]{:S(2)}) copy-start(bf16[128,128]{1,0:T(8,128)(2,1)} %rows_ref.1) | copy-start | bytes 98308
  2.0 21.2 %copy-start.1 = (bf16[128,128]{1,0:T(8,128)(2,1)S(1)}, bf16[128,128]{1,0:T(8,128)(2,1)}, u32[]{:S(2)}) copy-start(bf16[128,128]{1,0:T(8,128)(2,1)} %cols_ref.1) | copy-start | bytes 98308
  2.1 25.5 %all-to-all-start = ((bf16[32,32,128]{2,1,0:T(8,128)(2,1)}), bf16[32,32,128]{2,1,0:T(8,128)(2,1)S(1)}, u32[]{:S(2)}, u32[]{:S(2)}) async-start(bf16[32,32,128]{2,1,0:T(8,128)(2,1)} %bitcast.23), calls=%async_computation | async-start | bytes 524288 | tf_op jit(solution)/shard_map/all_to_all | solution.py:163
  23.2 0.7 copy-start.2
  23.2 0.7 copy-start.3
  23.2 0.7 copy-start.4

commit v7 on v6

--- a/solution.py
+++ b/solution.py
@@ -42,7 +42,7 @@
     return jnp.dot(a, b, preferred_element_type=F32)
 
 
-def tables_kernel(band_ref, weight_ref, ray_ref, rows_ref, cols_ref, mix_ref, smooth_ref, wide_ref):
+def fill_tables(band_ref, weight_ref, ray_ref, rows_ref, cols_ref, mix_ref, smooth_ref, wide_ref):
     count = SHELL * PER
     band = count // 2
     core = lax.axis_index("core")
@@ -82,33 +82,34 @@
     return [jnp.concatenate([s[:, k * PART : (k + 1) * PART] for s in slabs], axis=1) for k in range(X)]
 
 
-def send_kernel(rays_ref, out_ref, rays, slabs, arrived, left):
+def open_kernel(*refs):
+    given, rays_ref = refs[:5], refs[5]
+    tables, out_ref = refs[6:9], refs[9]
+    held, rays, arrived = refs[10:15], refs[15], refs[16]
     cut = Z0 * Y * PER
-    pieces = ((cut, 0, LINES - cut), (0, LINES - cut, cut))
+    small = [pltpu.make_async_copy(src, dst, arrived.at[k]) for k, (src, dst) in enumerate(zip(given, held))]
     reads = [
-        pltpu.make_async_copy(rays_ref.at[pl.ds(start, size)], rays.at[pl.ds(to, size)], arrived.at[k])
-        for k, (start, to, size) in enumerate(pieces)
+        pltpu.make_async_copy(rays_ref.at[pl.ds(start, size)], rays.at[pl.ds(to, size)], arrived.at[5 + k])
+        for k, (start, to, size) in enumerate(((cut, 0, LINES - cut), (0, LINES - cut, cut)))
     ]
-    for read in reads:
+    for read in small + reads:
         read.start()
     to, at = iota((SIDE, SIDE), 0), iota((SIDE, SIDE), 1)
     run = ZR * PER
     order = one_hot(at == to % run // PER * (Y * PER) + (to // run + Y0) % Y * PER + to % PER)
+    for read in small:
+        read.wait()
+    fill_tables(*held, *tables)
     for read in reads:
         read.wait()
     wide = jnp.concatenate([rays[k * SIDE : (k + 1) * SIDE] for k in range(X)], axis=1)
     turned = dot(order, wide)
     parts = swap([turned[:, k * SIDE : (k + 1) * SIDE] for k in range(X)])
-    writes = []
     for x in range(X):
-        slabs[x * SIDE : (x + 1) * SIDE] = parts[(x + X0) % X].astype(BF16)
+        slab = parts[(x + X0) % X].astype(BF16)
         for core in range(CORE):
-            k = x * CORE + core
-            source = slabs.at[pl.ds(x * SIDE, SIDE)]
-            writes.append(pltpu.make_async_copy(source, out_ref.at[pl.ds(k * SIDE, SIDE)], left.at[k]))
-            writes[-1].start()
-    for write in writes:
-        write.wait()
+            at_row = (x * CORE + core) * SIDE
+            out_ref[at_row : at_row + SIDE] = slab
 
 
 def mix_kernel(mix_ref, planes_ref, out_ref):
@@ -149,14 +150,12 @@
 
 def shards(residual, tile_ray, filter_rows, filter_cols, band_lo, shell_weight):
     tiles = Z * Y
-    mix, smooth, wide = call(
-        tables_kernel, "tables", [(SIDE, 2 * SIDE), (LINES, LINES), (LINES, LINES)],
-        band_lo.reshape(1, -1), shell_weight.reshape(1, -1), tile_ray.reshape(1, -1), filter_rows, filter_cols,
-    )
     rays = residual.reshape(PER, tiles, SIDE).transpose(1, 0, 2).reshape(LINES, SIDE)
-    (send,) = call(
-        send_kernel, "send", [(CORE * LINES, SIDE)], rays,
-        ins=HBM, outs=HBM, scratch=[SLAB, SLAB, dmas(2), dmas(SHELL)], params=WHOLE,
+    given = (band_lo.reshape(1, -1), shell_weight.reshape(1, -1), tile_ray.reshape(1, -1), filter_rows, filter_cols)
+    held = [pltpu.VMEM(arg.shape, arg.dtype) for arg in given]
+    mix, smooth, wide, send = call(
+        open_kernel, "open", [(SIDE, 2 * SIDE), (LINES, LINES), (LINES, LINES), (CORE * LINES, SIDE)], *[pltpu.with_memory_space_constraint(arg, pltpu.HBM) for arg in (*given, rays)],
+        ins=HBM, scratch=[*held, SLAB, dmas(7)],
     )
     peers = SHELL * Y
     near = [[((X0 + x) % X * CORE + c) * Y + (Y0 + y) % Y for x in range(X) for c in range(CORE) for y in range(Y)]]

time: 69.2 us -> 68.5 us (0.990)
  blocking collectives: 39.9 us -> 64.8 us
  starting transfers between devices: 21.1 us -> 0 us
  waiting for transfers between devices: 2.9 us -> 0 us
  Pallas kernels: 4.24 us -> 3.48 us
    all_to_all x0 -> x1, blocking collectives: none -> 25.2 us  [shards(): lax.all_to_all(send.reshape(peers, -1, SIDE), ('x', 'core', 'y'), 0, 0, a...]
    all_to_all x1 -> x0, starting transfers between devices: 21.1 us -> none  [shards(): lax.all_to_all(send.reshape(peers, -1, SIDE), ('x', 'core', 'y'), 0, 0, a...]
    all_to_all x1 -> x0, waiting for transfers between devices: 2.9 us -> none  [shards(): lax.all_to_all(send.reshape(peers, -1, SIDE), ('x', 'core', 'y'), 0, 0, a...]
    pallas_call x4 -> x3, Pallas kernels: 4.24 us -> 3.48 us  [call(): pl.pallas_call(kernel, out_shape=out_shape, compiler_params=params, name=...]
  transfers between devices with their start and end apart: 1 -> 0, of which waited for: 1 -> 0; matrix products, arithmetic and copies ran while one was open for 0% -> 0% of each run, Pallas kernels for 1% -> 0%
where the time goes in v7:
time: 68.5 us; the launch traced here: 68.3 us
  blocking collectives  64.8 us (95%)
  Pallas kernels  3.48 us (5%)
    all_to_all x1, blocking collectives, shards(): lax.all_to_all(mixed.reshape(X * Z, PER, SIDE), ('x', 'z'), 0, 0, axis_in...  39.6 us
    all_to_all x1, blocking collectives, shards(): lax.all_to_all(send.reshape(peers, -1, SIDE), ('x', 'core', 'y'), 0, 0, a...  25.2 us
    pallas_call x3, Pallas kernels, call(): pl.pallas_call(kernel, out_shape=out_shape, compiler_params=params, name=...  3.48 us

profile of v7, /device:TPU:1, one launch (start us, length us, event | category | flops | bytes accessed | tf_op | source)
XLA Modules:
  0.0 68.3 jit_solution(7836092285544643021)
XLA Ops:
  0.0 2.0 %open.1 = (bf16[128,256]{1,0:T(8,128)(2,1)S(1)}, bf16[512,512]{1,0:T(8,128)(2,1)S(1)}, bf16[512,512]{1,0:T(8,128)(2,1)S(1)}, bf16[1024,128]{1,0:T(8,128)(2,1)S(1)}) custom-call(s32[1,32]{1,0:T(1,128)} %bitcast.22, f32[1,32]{1,0:T(1,128)} %bitcast.23, s32[1,128]{1,0:T(1,128)} %bitcast.24, bf16[128,128]{1,0:T(8,128)(2,1)} %refs_3_.1, ...), custom_call_target="tpu_custom_call" | custom-call | tf_op jit(solution)/shard_map/open/pallas_call | solution.py:148
  2.0 25.2 %all_to_all.10 = bf16[32,32,128]{2,1,0:T(8,128)(2,1)S(1)} all-to-all(bf16[32,32,128]{2,1,0:T(8,128)(2,1)S(1)} %bitcast.20), channel_id=1, replica_groups={{514,515,512,513,642,643,640,641,770,771,768,769,898,899,896,897,2,3,0,..., dimensions={0} | all-to-all | bytes 524288 | tf_op jit(solution)/shard_map/all_to_all | solution.py:162
  27.3 0.3 mix.1
  27.6 39.6 %all_to_all.11 = bf16[128,4,128]{2,1,0:T(4,128)(2,1)S(1)} all-to-all(bf16[128,4,128]{2,1,0:T(4,128)(2,1)S(1)} %bitcast.19), channel_id=1, replica_groups={{580,584,588,592,596,600,604,608,612,616,620,624,628,632,636,512,516,52..., dimensions={0} | all-to-all | bytes 262144 | tf_op jit(solution)/shard_map/all_to_all | solution.py:167
  67.2 1.1 %smooth.1 = bf16[512,128]{1,0:T(8,128)(2,1)} custom-call(bf16[512,512]{1,0:T(8,128)(2,1)S(1)} %get-tuple-element.9.smooth_ref, bf16[512,512]{1,0:T(8,128)(2,1)S(1)} %get-tuple-element.10.wide_ref, bf16[512,128]{1,0:T(8,128)(2,1)S(1)} %bitcast.18), custom_call_target="tpu_custom_call" | custom-call | tf_op jit(solution)/shard_map/smooth/pallas_call | solution.py:148

commit v8 on v7

--- a/solution.py
+++ b/solution.py
@@ -20,7 +20,7 @@
 PART = SIDE // X
 ZR = Z // X
 LINES = PER * Z * Y
-X0, Y0, Z0 = 2, 2, 17
+X0, Y0, Z0 = 2, 2, 18
 
 
 SLAB = pltpu.VMEM((LINES, SIDE), BF16)
@@ -42,10 +42,24 @@
     return jnp.dot(a, b, preferred_element_type=F32)
 
 
-def fill_tables(band_ref, weight_ref, ray_ref, rows_ref, cols_ref, mix_ref, smooth_ref, wide_ref):
-    count = SHELL * PER
+def patterns():
+    count, part = SHELL * PER, ZR * PER
+    core = lax.axis_index("core")
+    spot, which = iota((X * part, count), 0), iota((X * part, count), 1)
+    pick_out = one_hot(which == ((spot // part + X0) % X * CORE + core) * PER + spot % PER)
+    spot, which = iota((SHELL * part, count), 0), iota((SHELL * part, count), 1)
+    source = (spot // (CORE * part) + X0) % X * CORE + spot // part % CORE
+    pick_in = one_hot(which == source * PER + spot % PER)
+    line, lane = iota((LINES, SIDE), 0), iota((LINES, SIDE), 1)
+    pixel = one_hot(lane == line // PER)
+    column = one_hot(lane == (line // SIDE + X0) % X * PART + line % PART)
+    return pick_out, pick_in, pixel, column
+
+
+def fill_tables(ready, band_ref, weight_ref, ray_ref, rows_ref, cols_ref, mix_ref, smooth_ref, wide_ref):
+    pick_out, pick_in, pixel, column = ready
+    count, part = SHELL * PER, ZR * PER
     band = count // 2
-    core = lax.axis_index("core")
     shell, plane = iota((count, count), 0), iota((count, count), 1)
     low = jnp.broadcast_to(band_ref[...], (count, count))
     lanes = jnp.broadcast_to(weight_ref[...], (count, count))
@@ -55,25 +69,18 @@
     values = 8.0 * weight * chi_shell * (chi_source - chi_shell) / chi_source
     inside = (shell >= low) & (shell < low + band)
     table = jnp.where(inside, values, 0.0).astype(BF16)
-
-    part = ZR * PER
-    spot, which = iota((X * part, count), 0), iota((X * part, count), 1)
-    pick_out = one_hot(which == ((spot // part + X0) % X * CORE + core) * PER + spot % PER)
-    spot, which = iota((SHELL * part, count), 0), iota((SHELL * part, count), 1)
-    source = (spot // (CORE * part) + X0) % X * CORE + spot // part % CORE
-    pick_in = one_hot(which == source * PER + spot % PER)
     full = lax.dot_general(dot(pick_out, table).astype(BF16), pick_in, ROW_BY_ROW, preferred_element_type=F32)
     here, there = iota(full.shape, 0), iota(full.shape, 1)
     mix_ref[...] = jnp.where(here % part // PER == there % part // PER, full, 0.0).astype(BF16)
 
-    line, lane = iota((LINES, SIDE), 0), iota((LINES, SIDE), 1)
-    spread = lax.dot_general(one_hot(lane == line // PER), rows_ref[...], ROW_BY_ROW, preferred_element_type=F32).astype(BF16)
+    line = iota((LINES, SIDE), 0)
+    spread = lax.dot_general(pixel, rows_ref[...], ROW_BY_ROW, preferred_element_type=F32).astype(BF16)
     block = (line % SIDE // PER + Z0) % Z * Y + (line // SIDE + Y0) % Y
     product = lax.dot_general(spread, one_hot(ray_ref[...] == block), ROW_BY_ROW, preferred_element_type=F32)
     here, there = iota((LINES, LINES), 0), iota((LINES, LINES), 1)
     smooth_ref[...] = jnp.where(here % PER == there % PER, product, 0.0).astype(BF16)
 
-    cols = dot(one_hot(lane == (line // SIDE + X0) % X * PART + line % PART), cols_ref[...])
+    cols = dot(column, cols_ref[...])
     for y in range(Y):
         wide_ref[:, y * SIDE : (y + 1) * SIDE] = jnp.where(line % SIDE // PART == y, cols, 0.0).astype(BF16)
 
@@ -97,9 +104,10 @@
     to, at = iota((SIDE, SIDE), 0), iota((SIDE, SIDE), 1)
     run = ZR * PER
     order = one_hot(at == to % run // PER * (Y * PER) + (to // run + Y0) % Y * PER + to % PER)
+    ready = patterns()
     for read in small:
         read.wait()
-    fill_tables(*held, *tables)
+    fill_tables(ready, *held, *tables)
     for read in reads:
         read.wait()
     wide = jnp.concatenate([rays[k * SIDE : (k + 1) * SIDE] for k in range(X)], axis=1)

time: 68.5 us -> 68.2 us (level)
  no operation moved by 1% of the time
where the time goes in v8:
time: 68.2 us; the launch traced here: 68 us
  blocking collectives  64.6 us (95%)
  Pallas kernels  3.34 us (5%)
    all_to_all x1, blocking collectives, shards(): lax.all_to_all(mixed.reshape(X * Z, PER, SIDE), ('x', 'z'), 0, 0, axis_in...  39.4 us
    all_to_all x1, blocking collectives, shards(): lax.all_to_all(send.reshape(peers, -1, SIDE), ('x', 'core', 'y'), 0, 0, a...  25.2 us
    pallas_call x3, Pallas kernels, call(): pl.pallas_call(kernel, out_shape=out_shape, compiler_params=params, name=...  3.34 us

profile of v8, /device:TPU:1, one launch (start us, length us, event | category | flops | bytes accessed | tf_op | source)
XLA Modules:
  0.0 68.0 jit_solution(11247656654321138446)
XLA Ops:
  0.0 1.9 %open.1 = (bf16[128,256]{1,0:T(8,128)(2,1)S(1)}, bf16[512,512]{1,0:T(8,128)(2,1)S(1)}, bf16[512,512]{1,0:T(8,128)(2,1)S(1)}, bf16[1024,128]{1,0:T(8,128)(2,1)S(1)}) custom-call(s32[1,32]{1,0:T(1,128)} %bitcast.22, f32[1,32]{1,0:T(1,128)} %bitcast.23, s32[1,128]{1,0:T(1,128)} %bitcast.24, bf16[128,128]{1,0:T(8,128)(2,1)} %refs_3_.1, ...), custom_call_target="tpu_custom_call" | custom-call | tf_op jit(solution)/shard_map/open/pallas_call | solution.py:156
  1.9 25.2 %all_to_all.10 = bf16[32,32,128]{2,1,0:T(8,128)(2,1)S(1)} all-to-all(bf16[32,32,128]{2,1,0:T(8,128)(2,1)S(1)} %bitcast.20), channel_id=1, replica_groups={{514,515,512,513,642,643,640,641,770,771,768,769,898,899,896,897,2,3,0,..., dimensions={0} | all-to-all | bytes 524288 | tf_op jit(solution)/shard_map/all_to_all | solution.py:170
  27.1 0.3 mix.1
  27.5 39.4 %all_to_all.11 = bf16[128,4,128]{2,1,0:T(4,128)(2,1)S(1)} all-to-all(bf16[128,4,128]{2,1,0:T(4,128)(2,1)S(1)} %bitcast.19), channel_id=1, replica_groups={{584,588,592,596,600,604,608,612,616,620,624,628,632,636,512,516,520,52..., dimensions={0} | all-to-all | bytes 262144 | tf_op jit(solution)/shard_map/all_to_all | solution.py:175
  66.9 1.1 %smooth.1 = bf16[512,128]{1,0:T(8,128)(2,1)} custom-call(bf16[512,512]{1,0:T(8,128)(2,1)S(1)} %get-tuple-element.9.smooth_ref, bf16[512,512]{1,0:T(8,128)(2,1)S(1)} %get-tuple-element.10.wide_ref, bf16[512,128]{1,0:T(8,128)(2,1)S(1)} %bitcast.18), custom_call_target="tpu_custom_call" | custom-call | tf_op jit(solution)/shard_map/smooth/pallas_call | solution.py:156
